TPU v7x, 512 devices: a whole 4x8x8 slice. The times are simulated.
512 devices in a mesh: row: 16 (over x, y_lo), col: 16 (over z, core), dp: 2 (over y_hi).
Axes of the slice: x: 4, y: 8 (y_hi: 2, y_lo: 4; y = y_hi * 4 + y_lo), z: 8, core: 2. Of those that a mesh axis runs over, the one named last changes fastest.
Arguments:
- grad_output: bfloat16 [2, 2048, 8192], P('dp', 'col', 'row'), may hold values from -0.09375 to 0.09375
- block_input: bfloat16 [2, 2048, 8192], P('dp', 'col', 'row'), may hold values from -6 to 6
- query_branch: bfloat16 [2, 2048, 8192], P('dp', 'row', 'col'), may hold values from -6 to 6
- key_branch: bfloat16 [2, 2048, 8192], P('dp', 'row', 'col'), may hold values from -6 to 6
- value_branch: bfloat16 [2, 2048, 8192], P('dp', 'row', 'col'), may hold values from -6 to 6
- out_weight: bfloat16 [8192, 8192], P('row', 'col'), may hold values from -0.0625 to 0.0625
- filters: float32 [512, 128], P('col'), may hold values from -0.5 to 0.5
Outputs:
- out_weight_grad: float32 [8192, 8192], P('row', 'col')
- value_weight_grad: float32 [8192, 8192], P('col', 'row')
- filter_grad: float32 [512, 128], P('col')
All inputs are finite; a program needn't handle non-finite values.
Results may differ from a plain program's by a relative error of at most 0.0029.
Values may be sent and summed in bfloat16 or wider, within the bound.
A program may use at most 128 MiB of HBM per device.

v0:
```python
import jax
import jax.numpy as jnp
from jax import lax
from jax.sharding import PartitionSpec as P

highest = lax.Precision.HIGHEST


def toeplitz(taps, tok_rows, causal):
    filter_len = taps.shape[1]
    out_pos = lax.broadcasted_iota(jnp.int32, (tok_rows, tok_rows + filter_len), 0)
    in_pos = lax.broadcasted_iota(jnp.int32, (tok_rows, tok_rows + filter_len), 1)
    lagged = out_pos + filter_len - in_pos if causal else in_pos - out_pos
    inside = (lagged >= 0) & (lagged < filter_len)
    picked = jnp.take(taps, jnp.clip(lagged, 0, filter_len - 1), axis=1)
    return jnp.where(inside[None], picked, 0.0)


def grouped_apply(table, signal, groups):
    blocks, extent, channels = signal.shape
    split = signal.reshape(blocks, extent, groups, channels // groups)
    result = jnp.einsum("gts,bsgc->btgc", table, split, precision=highest)
    return result.reshape(blocks, table.shape[1], channels)


def taps_partial(delta_mix, mixed_ext, groups, filter_len):
    blocks, tok_rows, channels = delta_mix.shape
    left_side = delta_mix.reshape(blocks, tok_rows, groups, channels // groups)
    right_side = mixed_ext.reshape(blocks, tok_rows + filter_len, groups, channels // groups)
    products = jnp.einsum("btgc,bsgc->gts", left_side, right_side, precision=highest)
    extent = tok_rows + filter_len
    flipped = products[:, :, ::-1]
    padded = jnp.pad(flipped, ((0, 0), (0, 0), (0, tok_rows)))
    flat_rows = padded.reshape(groups, -1)[:, : tok_rows * (extent + tok_rows - 1)]
    skewed = flat_rows.reshape(groups, tok_rows, extent + tok_rows - 1)
    column_sums = jnp.sum(skewed, axis=1)
    return column_sums[:, tok_rows - 1 : tok_rows - 1 + filter_len]


def local(grad_output, block_input, query_branch, key_branch, value_branch, out_weight, filters):
    filter_len = filters.shape[1]
    groups = filters.shape[0]
    tok_rows = query_branch.shape[1]
    channels = query_branch.shape[2]
    grads_all, inputs_all = (
        lax.all_gather(grad_output[0], "col", axis=0, tiled=True),
        lax.all_gather(block_input[0], "col", axis=0, tiled=True),
    )
    row_devices = lax.axis_size("row")
    sub_width = channels // row_devices
    delta_turned = lax.psum_scatter(
        lax.dot_general(
            out_weight, grads_all, (((0,), (1,)), ((), ())), preferred_element_type=jnp.float32
        ),
        "row",
        scatter_dimension=0,
        tiled=True,
    )
    queries, keys_here, values_here = (
        lax.all_to_all(query_branch[0], "row", split_axis=1, concat_axis=0, tiled=True),
        lax.all_to_all(key_branch[0], "row", split_axis=1, concat_axis=0, tiled=True),
        lax.all_to_all(value_branch[0], "row", split_axis=1, concat_axis=0, tiled=True),
    )
    delta_out = delta_turned.T
    local_groups = sub_width // (channels // groups)
    first_group = lax.axis_index("row") * local_groups
    my_taps = lax.dynamic_slice_in_dim(filters, first_group, local_groups, 0)
    mixed = keys_here.astype(jnp.float32) * values_here.astype(jnp.float32)
    mixed_blocks = mixed.reshape(row_devices, tok_rows, sub_width)
    earlier = jnp.concatenate(
        [
            jnp.zeros((1, filter_len, sub_width), jnp.float32),
            mixed_blocks[:-1, tok_rows - filter_len :],
        ],
        axis=0,
    )
    mixed_ext = jnp.concatenate([earlier, mixed_blocks], axis=1)
    conv_out = grouped_apply(toeplitz(my_taps, tok_rows, True), mixed_ext, local_groups).reshape(
        -1, sub_width
    )
    gated = (queries.astype(jnp.float32) * conv_out).astype(jnp.bfloat16)
    delta_mix = delta_out * queries.astype(jnp.float32)
    delta_blocks = delta_mix.reshape(row_devices, tok_rows, sub_width)
    later_part = jnp.concatenate(
        [delta_blocks[1:, :filter_len], jnp.zeros((1, filter_len, sub_width), jnp.float32)], axis=0
    )
    delta_ext = jnp.concatenate([delta_blocks, later_part], axis=1)
    delta_conv = grouped_apply(toeplitz(my_taps, tok_rows, False), delta_ext, local_groups).reshape(
        -1, sub_width
    )
    delta_value = (delta_conv * keys_here.astype(jnp.float32)).astype(jnp.bfloat16)
    my_terms = taps_partial(delta_blocks, mixed_ext, local_groups, filter_len)
    taps_local = lax.dynamic_update_slice_in_dim(
        jnp.zeros(filters.shape, jnp.float32), my_terms, first_group, 0
    )
    gated_all, value_all = (
        lax.all_gather(gated, "row", axis=1, tiled=True),
        lax.all_gather(delta_value, "row", axis=1, tiled=True),
    )
    out_grad = lax.dot_general(
        grads_all, gated_all, (((0,), (0,)), ((), ())), preferred_element_type=jnp.float32
    )
    value_grad = lax.dot_general(
        value_all, inputs_all, (((0,), (0,)), ((), ())), preferred_element_type=jnp.float32
    )
    out_grad, value_grad = lax.psum((out_grad, value_grad), "dp")
    taps_total = lax.psum(taps_local, ("row", "dp"))
    return (out_grad, value_grad, taps_total)


def solution(mesh):
    in_specs = (
        P("dp", "col", "row"),
        P("dp", "col", "row"),
        P("dp", "row", "col"),
        P("dp", "row", "col"),
        P("dp", "row", "col"),
        P("row", "col"),
        P("col", None),
    )
    out_specs = (P("row", "col"), P("col", "row"), P("col", None))
    return jax.shard_map(local, mesh=mesh, in_specs=in_specs, out_specs=out_specs, check_vma=False)
```

profile of v0, /device:TPU:64, one launch (start us, length us, event | category | flops | bytes accessed | tf_op | source)
XLA Modules:
  0.0 689.4 jit_solution(379694975442089937)
XLA Ops:
  7.2 0.7 all-gather.11.cloned.1.call-update
  8.0 48.5 %all-gather.11.cloned.1.call-done = bf16[1,2048,512]{2,1,0:T(8,128)(2,1)} async-done(((bf16[1,128,512]{2,1,0:T(8,128)(2,1)}), bf16[1,2048,512]{2,1,0:T(8,128)(2,1)}) %all-gather.11.cloned.1.call-update) | async-done | bytes 2097168 | tf_op jit(solution)/shard_map/all_gather | solution.py:46
  56.5 4.8 fusion.2
  61.4 0.9 copy-done.2
  62.2 0.8 copy.40
  63.0 7.1 %all-to-all-start.2 = ((bf16[128,16,32]{0,2,1:T(8,128)(2,1)}), bf16[128,16,32]{0,2,1:T(8,128)(2,1)S(1)}, u32[]{:S(2)}, u32[]{:S(2)}) async-start(bf16[128,16,32]{0,2,1:T(8,128)(2,1)} %bitcast.4), calls=%async_computation.2 | async-start | bytes 262144 | tf_op jit(solution)/shard_map/all_to_all | solution.py:62
  70.1 0.1 fusion.30
  70.3 0.1 copy.66
  70.4 0.7 constant_dynamic-slice_fusion
  71.1 0.8 copy.38
  71.8 0.1 copy.62
  71.9 109.0 %gather_fusion = f32[32768,2]{1,0:T(8,128)} fusion(f32[2,128]{0,1:T(8,128)S(1)} %copy.62, s32[32768]{0:T(1024)S(1)} %broadcast_clamp_fusion.1), kind=kCustom, calls=%fused_computation.clone | custom fusion | bytes 655360 | tf_op jit(solution)/shard_map/jit(_take)/gather | solution.py:15
  180.9 10.0 %copy.46 = f32[128,256,2]{1,0,2:T(8,128)S(1)} copy(f32[128,256,2]{2,1,0:T(8,128)} %bitcast.113) | data formatting | bytes 524288 | tf_op jit(solution)/shard_map/jit(_take)/gather | solution.py:15
  190.9 0.8 copy.36
  191.7 0.2 fusion.35
  191.9 7.5 %all-to-all-start.1 = ((bf16[128,16,32]{0,2,1:T(8,128)(2,1)}), bf16[128,16,32]{0,2,1:T(8,128)(2,1)S(1)}, u32[]{:S(2)}, u32[]{:S(2)}) async-start(bf16[128,16,32]{0,2,1:T(8,128)(2,1)} %bitcast.2), calls=%async_computation.1 | async-start | bytes 262144 | tf_op jit(solution)/shard_map/all_to_all | solution.py:61
  199.4 8.4 %all-to-all-done.1 = bf16[128,16,32]{0,2,1:T(8,128)(2,1)S(1)} async-done(((bf16[128,16,32]{0,2,1:T(8,128)(2,1)}), bf16[128,16,32]{0,2,1:T(8,128)(2,1)S(1)}, u32[]{:S(2)}, u32[]{:S(2)}) %all-to-all-start.1) | async-done | bytes 131104 | tf_op jit(solution)/shard_map/all_to_all | solution.py:61
  207.8 3.5 all-to-all-start
  211.3 0.0 all-gather.7.cloned.1.call-start
  211.4 0.1 slice.19
  211.5 0.1 copy_dynamic-update-slice_fusion
  211.7 0.6 convolution_bitcast_fusion.2
  212.3 0.1 copy.47
  212.4 7.3 %all-to-all-done = bf16[128,16,32]{0,2,1:T(8,128)(2,1)S(1)} async-done(((bf16[128,16,32]{0,2,1:T(8,128)(2,1)}), bf16[128,16,32]{0,2,1:T(8,128)(2,1)S(1)}, u32[]{:S(2)}, u32[]{:S(2)}) %all-to-all-start) | async-done | bytes 131104 | tf_op jit(solution)/shard_map/all_to_all | solution.py:60
  219.6 1.7 bitcast_multiply_fusion.2
  221.4 0.5 all-gather.13.cloned.1.call-update
  222.0 0.1 copy.69
  222.2 109.0 %gather_fusion.1 = f32[32768,2]{1,0:T(8,128)} fusion(f32[2,128]{0,1:T(8,128)S(1)} %copy.62, s32[32768]{0:T(1024)S(1)} %broadcast_clamp_fusion), kind=kCustom, calls=%fused_computation.1.clone | custom fusion | bytes 655360 | tf_op jit(solution)/shard_map/jit(_take)/gather | solution.py:15
  331.2 10.1 %copy.51 = f32[128,256,2]{1,0,2:T(8,128)S(1)} copy(f32[128,256,2]{2,1,0:T(8,128)} %bitcast.112) | data formatting | bytes 524288 | tf_op jit(solution)/shard_map/jit(_take)/gather | solution.py:15
  341.2 0.1 fusion.34
  341.3 0.1 slice.21
  341.4 0.1 copy.50
  341.6 0.1 copy.49
  341.7 0.6 convolution_bitcast_fusion.1
  342.3 0.1 copy.52
  342.4 0.7 fusion.13
  343.2 4.5 fusion.6
  347.7 1.5 all-gather.13.cloned.1.call-done
  349.2 91.4 %all-gather.9.cloned.1.call-done = bf16[2048,512]{0,1:T(8,128)(2,1)} async-done(((bf16[2048,32]{0,1:T(8,128)(2,1)}), bf16[2048,512]{0,1:T(8,128)(2,1)}) %all-gather.9.cloned.1.call-update) | async-done | bytes 2097168 | tf_op jit(solution)/shard_map/all_gather | solution.py:98
  440.6 4.4 fusion
  445.1 0.8 convolution_bitcast_fusion
  445.9 0.4 rev.3
  446.3 0.3 copy.71
  446.7 0.6 reshape.76
  447.3 0.1 slice_dynamic-update-slice_fusion
  447.4 231.5 %psum.23 = f32[32,128]{1,0:T(8,128)} all-reduce(f32[32,128]{1,0:T(8,128)S(1)} %slice_dynamic-update-slice_fusion), channel_id=1, replica_groups=mesh['row'=16,'col'=16,'dp'=2] {'row','dp'}, use_global_device_ids=true, to_apply=%region_4.6 | all-reduce | flops 4096 | bytes 32768 | tf_op jit(solution)/shard_map/psum | solution.py:107
  678.9 2.6 copy.54
  681.5 1.0 copy.88
  (39 shorter events, 0.7 us)
Async XLA Ops:
  7.2 49.3 %copy-start = (bf16[512,512]{1,0:T(8,128)(2,1)S(1)}, bf16[512,512]{1,0:T(8,128)(2,1)}, u32[]{:S(2)}) copy-start(bf16[512,512]{1,0:T(8,128)(2,1)} %param.14) | copy-start | bytes 1572868
  7.2 49.3 %all-gather.11.cloned.1.call-start = ((), (), s32[]{:S(2)}) async-start(), calls=%async_computation.7 | async-start | bytes 2228224 | tf_op jit(solution)/shard_map/all_gather | solution.py:46
  7.9 211.7 %reduce-scatter.2.cloned.1.call-start = ((), (), s32[]{:S(2)}) async-start(), calls=%async_computation.5 | async-start | bytes 4456448 | tf_op jit(solution)/shard_map/reduce_scatter | solution.py:51
  61.3 0.9 copy-start.2
  61.3 9.7 %copy-start.3 = (bf16[1,128,512]{2,1,0:T(8,128)(2,1)S(1)}, bf16[1,128,512]{2,1,0:T(8,128)(2,1)}, u32[]{:S(2)}) copy-start(bf16[1,128,512]{2,1,0:T(8,128)(2,1)} %param.12) | copy-start | bytes 393220
  63.0 128.9 %all-to-all-start.2 = ((bf16[128,16,32]{0,2,1:T(8,128)(2,1)}), bf16[128,16,32]{0,2,1:T(8,128)(2,1)S(1)}, u32[]{:S(2)}, u32[]{:S(2)}) async-start(bf16[128,16,32]{0,2,1:T(8,128)(2,1)} %bitcast.4), calls=%async_computation.2 | async-start | bytes 262144 | tf_op jit(solution)/shard_map/all_to_all | solution.py:62
  180.9 10.0 %copy-start.4 = (bf16[1,128,512]{2,1,0:T(8,128)(2,1)S(1)}, bf16[1,128,512]{2,1,0:T(8,128)(2,1)}, u32[]{:S(2)}) copy-start(bf16[1,128,512]{2,1,0:T(8,128)(2,1)} %param.11) | copy-start | bytes 393220
  191.9 15.9 %all-to-all-start.1 = ((bf16[128,16,32]{0,2,1:T(8,128)(2,1)}), bf16[128,16,32]{0,2,1:T(8,128)(2,1)S(1)}, u32[]{:S(2)}, u32[]{:S(2)}) async-start(bf16[128,16,32]{0,2,1:T(8,128)(2,1)} %bitcast.2), calls=%async_computation.1 | async-start | bytes 262144 | tf_op jit(solution)/shard_map/all_to_all | solution.py:61
  207.8 11.9 %all-to-all-start = ((bf16[128,16,32]{0,2,1:T(8,128)(2,1)}), bf16[128,16,32]{0,2,1:T(8,128)(2,1)S(1)}, u32[]{:S(2)}, u32[]{:S(2)}) async-start(bf16[128,16,32]{0,2,1:T(8,128)(2,1)} %bitcast), calls=%async_computation | async-start | bytes 262144 | tf_op jit(solution)/shard_map/all_to_all | solution.py:60
  211.3 131.9 %all-gather.7.cloned.1.call-start = ((), (), s32[]{:S(2)}) async-start(), calls=%async_computation.4 | async-start | bytes 2228224 | tf_op jit(solution)/shard_map/all_gather | solution.py:97
  221.4 127.9 %all-gather.13.cloned.1.call-start = ((), (), s32[]{:S(2)}) async-start(), calls=%async_computation.8 | async-start | bytes 2228224 | tf_op jit(solution)/shard_map/all_gather | solution.py:47
  222.0 218.7 %all-gather.9.cloned.1.call-start = ((), (), s32[]{:S(2)}) async-start(), calls=%async_computation.6 | async-start | bytes 2228224 | tf_op jit(solution)/shard_map/all_gather | solution.py:98
  343.2 335.8 %all-reduce.6.cloned.1.call-start = ((), (), s32[]{:S(2)}) async-start(), calls=%async_computation.9 | async-start | bytes 4194304 | tf_op jit(solution)/shard_map/psum | solution.py:106
  678.9 2.6 copy-start.1
Sparse Core Ops, SparseCore 0:
  10.1 46.3 all-gather.10
  61.5 105.1 reduce-scatter.1
  221.5 84.2 all-gather.6
  307.8 41.4 all-gather.12
  351.7 88.8 all-gather.8
  445.2 122.4 all-reduce.5
where the time goes:
time: 690 us; the launch traced here: 689 us
  local copies, waits for them, and re-layouts  248 us (36%)
  blocking collectives  232 us (34%)
  waiting for transfers between devices  158 us (23%)
  starting transfers between devices  18.4 us (3%)
  matrix products  15.8 us (2%)
  between operations  14.4 us (2%)
    gather x4, local copies, waits for them, and re-layouts, toeplitz(): picked = jnp.take(taps, jnp.clip(lagged, 0, filter_len - 1), axis=1)  238 us
    psum x1, blocking collectives, local(): taps_total = lax.psum(taps_local, ('row', 'dp'))  232 us
    all_gather x1, waiting for transfers between devices, local(): lax.all_gather(delta_value, 'row', axis=1, tiled=True)  91.4 us
    all_gather x1, waiting for transfers between devices, local(): lax.all_gather(grad_output[0], 'col', axis=0, tiled=True)  48.5 us
  transfers between devices with their start and end apart: 9, of which 5 were waited for; matrix products, arithmetic and copies ran while one was open for 36% of the time, Pallas kernels for 0%

commit v1 on v0

--- a/solution.py
+++ b/solution.py
@@ -104,7 +104,7 @@
         value_all, inputs_all, (((0,), (0,)), ((), ())), preferred_element_type=jnp.float32
     )
     out_grad, value_grad = lax.psum((out_grad, value_grad), "dp")
-    taps_total = lax.psum(taps_local, ("row", "dp"))
+    taps_total = lax.psum(lax.psum(taps_local, "row"), "dp")
     return (out_grad, value_grad, taps_total)
 
 

time: 690 us -> 588 us (0.85)
  the two profiles are of different devices: /device:TPU:64 before, /device:TPU:1 now
where the time goes in v1:
time: 588 us; the launch traced here: 587 us
  local copies, waits for them, and re-layouts  246 us (42%)
  waiting for transfers between devices  201 us (34%)
  blocking collectives  89.1 us (15%)
  starting transfers between devices  17.5 us (3%)
  matrix products  15.8 us (3%)
  between operations  14.4 us (2%)
    gather x4, local copies, waits for them, and re-layouts, toeplitz(): picked = jnp.take(taps, jnp.clip(lagged, 0, filter_len - 1), axis=1)  237 us
    psum x2, blocking collectives, local(): taps_total = lax.psum(lax.psum(taps_local, 'row'), 'dp')  89.1 us
    all_gather x1, waiting for transfers between devices, local(): lax.all_gather(delta_value, 'row', axis=1, tiled=True)  81.3 us
    all_gather x1, waiting for transfers between devices, local(): lax.all_gather(grad_output[0], 'col', axis=0, tiled=True)  51.3 us
    psum x1, waiting for transfers between devices, local(): out_grad, value_grad = lax.psum((out_grad, value_grad), 'dp')  47.8 us
  transfers between devices with their start and end apart: 9, of which 6 were waited for; matrix products, arithmetic and copies ran while one was open for 43% of the time, Pallas kernels for 0%

profile of v1, /device:TPU:1, one launch (start us, length us, event | category | flops | bytes accessed | tf_op | source)
XLA Modules:
  0.0 587.0 jit_solution(13863234167863108157)
XLA Ops:
  7.2 0.7 all-gather.11.cloned.1.call-update
  8.0 51.3 %all-gather.11.cloned.1.call-done = bf16[1,2048,512]{2,1,0:T(8,128)(2,1)} async-done(((bf16[1,128,512]{2,1,0:T(8,128)(2,1)}), bf16[1,2048,512]{2,1,0:T(8,128)(2,1)}) %all-gather.11.cloned.1.call-update) | async-done | bytes 2097168 | tf_op jit(solution)/shard_map/all_gather | solution.py:46
  59.3 4.8 fusion.2
  64.1 0.9 copy-done.2
  65.0 0.8 copy.40
  65.8 6.8 %all-to-all-start.2 = ((bf16[128,16,32]{0,2,1:T(8,128)(2,1)}), bf16[128,16,32]{0,2,1:T(8,128)(2,1)S(1)}, u32[]{:S(2)}, u32[]{:S(2)}) async-start(bf16[128,16,32]{0,2,1:T(8,128)(2,1)} %bitcast.4), calls=%async_computation.2 | async-start | bytes 262144 | tf_op jit(solution)/shard_map/all_to_all | solution.py:62
  72.6 0.1 fusion.30
  72.7 0.1 copy.66
  72.8 0.7 constant_dynamic-slice_fusion
  73.6 0.8 copy.38
  74.3 0.1 copy.62
  74.4 108.2 %gather_fusion = f32[32768,2]{1,0:T(8,128)} fusion(f32[2,128]{0,1:T(8,128)S(1)} %copy.62, s32[32768]{0:T(1024)S(1)} %broadcast_clamp_fusion.1), kind=kCustom, calls=%fused_computation.clone | custom fusion | bytes 655360 | tf_op jit(solution)/shard_map/jit(_take)/gather | solution.py:15
  182.7 10.0 %copy.46 = f32[128,256,2]{1,0,2:T(8,128)S(1)} copy(f32[128,256,2]{2,1,0:T(8,128)} %bitcast.113) | data formatting | bytes 524288 | tf_op jit(solution)/shard_map/jit(_take)/gather | solution.py:15
  192.6 0.8 copy.36
  193.4 0.2 fusion.35
  193.6 7.0 %all-to-all-start.1 = ((bf16[128,16,32]{0,2,1:T(8,128)(2,1)}), bf16[128,16,32]{0,2,1:T(8,128)(2,1)S(1)}, u32[]{:S(2)}, u32[]{:S(2)}) async-start(bf16[128,16,32]{0,2,1:T(8,128)(2,1)} %bitcast.2), calls=%async_computation.1 | async-start | bytes 262144 | tf_op jit(solution)/shard_map/all_to_all | solution.py:61
  200.6 7.2 %all-to-all-done.1 = bf16[128,16,32]{0,2,1:T(8,128)(2,1)S(1)} async-done(((bf16[128,16,32]{0,2,1:T(8,128)(2,1)}), bf16[128,16,32]{0,2,1:T(8,128)(2,1)S(1)}, u32[]{:S(2)}, u32[]{:S(2)}) %all-to-all-start.1) | async-done | bytes 131104 | tf_op jit(solution)/shard_map/all_to_all | solution.py:61
  207.8 3.5 all-to-all-start
  211.4 0.1 slice.19
  211.5 0.1 copy_dynamic-update-slice_fusion
  211.7 0.6 convolution_bitcast_fusion.2
  212.3 0.1 copy.47
  212.4 6.1 %all-to-all-done = bf16[128,16,32]{0,2,1:T(8,128)(2,1)S(1)} async-done(((bf16[128,16,32]{0,2,1:T(8,128)(2,1)}), bf16[128,16,32]{0,2,1:T(8,128)(2,1)S(1)}, u32[]{:S(2)}, u32[]{:S(2)}) %all-to-all-start) | async-done | bytes 131104 | tf_op jit(solution)/shard_map/all_to_all | solution.py:60
  218.5 1.7 bitcast_multiply_fusion.2
  220.3 0.5 all-gather.13.cloned.1.call-update
  220.9 0.1 copy.69
  221.0 108.2 %gather_fusion.1 = f32[32768,2]{1,0:T(8,128)} fusion(f32[2,128]{0,1:T(8,128)S(1)} %copy.62, s32[32768]{0:T(1024)S(1)} %broadcast_clamp_fusion), kind=kCustom, calls=%fused_computation.1.clone | custom fusion | bytes 655360 | tf_op jit(solution)/shard_map/jit(_take)/gather | solution.py:15
  329.3 10.1 %copy.51 = f32[128,256,2]{1,0,2:T(8,128)S(1)} copy(f32[128,256,2]{2,1,0:T(8,128)} %bitcast.112) | data formatting | bytes 524288 | tf_op jit(solution)/shard_map/jit(_take)/gather | solution.py:15
  339.3 0.1 fusion.34
  339.5 0.1 copy.50
  339.7 0.1 copy.49
  339.8 0.6 convolution_bitcast_fusion.1
  340.4 0.1 copy.52
  340.5 0.7 fusion.13
  341.3 4.5 fusion.6
  345.8 5.9 all-gather.13.cloned.1.call-done
  351.7 81.3 %all-gather.9.cloned.1.call-done = bf16[2048,512]{0,1:T(8,128)(2,1)} async-done(((bf16[2048,32]{0,1:T(8,128)(2,1)}), bf16[2048,512]{0,1:T(8,128)(2,1)}) %all-gather.9.cloned.1.call-update) | async-done | bytes 2097168 | tf_op jit(solution)/shard_map/all_gather | solution.py:98
  432.9 4.4 fusion
  437.4 0.8 convolution_bitcast_fusion
  438.2 0.4 rev.3
  438.7 0.3 copy.71
  439.0 0.6 reshape.76
  439.6 0.1 slice_dynamic-update-slice_fusion
  439.7 77.9 %psum.30 = f32[32,128]{1,0:T(8,128)S(1)} all-reduce(f32[32,128]{1,0:T(8,128)S(1)} %slice_dynamic-update-slice_fusion), channel_id=1, replica_groups=mesh['row'=16,'col'=16,'dp'=2] {'row'}, use_global_device_ids=true, to_apply=%region_4.6 | all-reduce | flops 4096 | bytes 32768 | tf_op jit(solution)/shard_map/psum | solution.py:107
  517.6 11.2 %psum.31 = f32[32,128]{1,0:T(8,128)} all-reduce(f32[32,128]{1,0:T(8,128)S(1)} %psum.30), channel_id=1, replica_groups=mesh['row'=16,'col'=16,'dp'=2] {'dp'}, use_global_device_ids=true, to_apply=%region_5.7 | all-reduce | flops 4096 | bytes 32768 | tf_op jit(solution)/shard_map/psum | solution.py:107
  528.8 47.8 %all-reduce.6.cloned.1.call-done = (f32[512,512]{0,1:T(8,128)}, f32[512,512]{1,0:T(8,128)}) async-done(((f32[512,512]{0,1:T(8,128)}, f32[512,512]{1,0:T(8,128)}), (f32[512,512]{0,1:T(8,128)}, f32[512,512]{1,0:T(8,128)})) %all-reduce.6.cloned.1.call-update) | async-done | bytes 2097168 | tf_op jit(solution)/shard_map/psum | solution.py:106
  576.6 2.6 copy.54
  579.2 1.0 copy.88
  (40 shorter events, 0.8 us)
Async XLA Ops:
  7.2 52.1 %copy-start = (bf16[512,512]{1,0:T(8,128)(2,1)S(1)}, bf16[512,512]{1,0:T(8,128)(2,1)}, u32[]{:S(2)}) copy-start(bf16[512,512]{1,0:T(8,128)(2,1)} %param.14) | copy-start | bytes 1572868
  7.2 52.1 %all-gather.11.cloned.1.call-start = ((), (), s32[]{:S(2)}) async-start(), calls=%async_computation.7 | async-start | bytes 2228224 | tf_op jit(solution)/shard_map/all_gather | solution.py:46
  7.9 210.6 %reduce-scatter.2.cloned.1.call-start = ((), (), s32[]{:S(2)}) async-start(), calls=%async_computation.5 | async-start | bytes 4456448 | tf_op jit(solution)/shard_map/reduce_scatter | solution.py:51
  64.1 0.9 copy-start.2
  64.1 9.4 %copy-start.3 = (bf16[1,128,512]{2,1,0:T(8,128)(2,1)S(1)}, bf16[1,128,512]{2,1,0:T(8,128)(2,1)}, u32[]{:S(2)}) copy-start(bf16[1,128,512]{2,1,0:T(8,128)(2,1)} %param.12) | copy-start | bytes 393220
  65.8 127.8 %all-to-all-start.2 = ((bf16[128,16,32]{0,2,1:T(8,128)(2,1)}), bf16[128,16,32]{0,2,1:T(8,128)(2,1)S(1)}, u32[]{:S(2)}, u32[]{:S(2)}) async-start(bf16[128,16,32]{0,2,1:T(8,128)(2,1)} %bitcast.4), calls=%async_computation.2 | async-start | bytes 262144 | tf_op jit(solution)/shard_map/all_to_all | solution.py:62
  182.6 10.0 %copy-start.4 = (bf16[1,128,512]{2,1,0:T(8,128)(2,1)S(1)}, bf16[1,128,512]{2,1,0:T(8,128)(2,1)}, u32[]{:S(2)}) copy-start(bf16[1,128,512]{2,1,0:T(8,128)(2,1)} %param.11) | copy-start | bytes 393220
  193.6 14.2 %all-to-all-start.1 = ((bf16[128,16,32]{0,2,1:T(8,128)(2,1)}), bf16[128,16,32]{0,2,1:T(8,128)(2,1)S(1)}, u32[]{:S(2)}, u32[]{:S(2)}) async-start(bf16[128,16,32]{0,2,1:T(8,128)(2,1)} %bitcast.2), calls=%async_computation.1 | async-start | bytes 262144 | tf_op jit(solution)/shard_map/all_to_all | solution.py:61
  207.8 10.7 %all-to-all-start = ((bf16[128,16,32]{0,2,1:T(8,128)(2,1)}), bf16[128,16,32]{0,2,1:T(8,128)(2,1)S(1)}, u32[]{:S(2)}, u32[]{:S(2)}) async-start(bf16[128,16,32]{0,2,1:T(8,128)(2,1)} %bitcast), calls=%async_computation | async-start | bytes 262144 | tf_op jit(solution)/shard_map/all_to_all | solution.py:60
  211.3 130.0 %all-gather.7.cloned.1.call-start = ((), (), s32[]{:S(2)}) async-start(), calls=%async_computation.4 | async-start | bytes 2228224 | tf_op jit(solution)/shard_map/all_gather | solution.py:97
  220.3 131.4 %all-gather.13.cloned.1.call-start = ((), (), s32[]{:S(2)}) async-start(), calls=%async_computation.8 | async-start | bytes 2228224 | tf_op jit(solution)/shard_map/all_gather | solution.py:47
  220.8 212.1 %all-gather.9.cloned.1.call-start = ((), (), s32[]{:S(2)}) async-start(), calls=%async_computation.6 | async-start | bytes 2228224 | tf_op jit(solution)/shard_map/all_gather | solution.py:98
  341.3 235.3 %all-reduce.6.cloned.1.call-start = ((), (), s32[]{:S(2)}) async-start(), calls=%async_computation.9 | async-start | bytes 4194304 | tf_op jit(solution)/shard_map/psum | solution.py:106
  576.6 2.6 copy-start.1
Sparse Core Ops, SparseCore 0:
  10.1 49.0 all-gather.10
  64.3 100.1 reduce-scatter.1
  220.4 77.4 all-gather.6
  299.9 51.7 all-gather.12
  354.2 78.7 all-gather.8
  437.5 138.9 all-reduce.5
